TPU v7x, 32 devices: a whole 2x2x4 slice. The times are simulated.
32 devices in a mesh: dp: 8 (over y, x, core), tensor: 4 (over z).
Axes of the slice: x: 2, y: 2, z: 4, core: 2. Of those that a mesh axis runs over, the one named last changes fastest.
Arguments:
- tokens: bfloat16 [8, 736, 1152], P('dp', 'tensor'), may hold values from -45 to 45
- key_mask: int32 [8, 736], P('dp'), may hold values from 0 to 1, as said below
- query_weight: bfloat16 [1152, 1152], P('dp', 'tensor'), may hold values from -0.1875 to 0.1875
- key_weight: bfloat16 [1152, 1152], P('dp', 'tensor'), may hold values from -0.1875 to 0.1875
- value_weight: bfloat16 [1152, 1152], P('dp', 'tensor'), may hold values from -0.1875 to 0.1875
- out_weight: bfloat16 [1152, 1152], P('tensor', 'dp'), may hold values from -0.375 to 0.375
- up_weight: bfloat16 [1152, 4304], P('dp', 'tensor'), may hold values from -0.1875 to 0.1875
- down_weight: bfloat16 [4304, 1152], P('tensor', 'dp'), may hold values from -0.09375 to 0.09375
- first_gain: bfloat16 [1152], P('dp'), may hold values from 0.5 to 1.5
- first_shift: bfloat16 [1152], P('dp'), may hold values from -3 to 3
- query_bias: bfloat16 [1152], P('dp'), may hold values from -3 to 3
- value_bias: bfloat16 [1152], P('dp'), may hold values from -3 to 3
- out_bias: bfloat16 [1152], P('dp'), may hold values from -3 to 3
- second_gain: bfloat16 [1152], P('dp'), may hold values from 0.5 to 1.5
- second_shift: bfloat16 [1152], P('dp'), may hold values from -3 to 3
- up_bias: bfloat16 [4304], P('dp'), may hold values from -3 to 3
- down_bias: bfloat16 [1152], P('dp'), may hold values from -3 to 3
- cotangent: bfloat16 [8, 736, 1152], P('dp', 'tensor'), may hold values from -6 to 6
Outputs:
- output: bfloat16 [8, 736, 1152], P('dp', 'tensor')
- input_grad: float32 [8, 736, 1152], P('dp', 'tensor')
- query_grad: float32 [1152, 1152], P('dp', 'tensor')
- key_grad: float32 [1152, 1152], P('dp', 'tensor')
- value_grad: float32 [1152, 1152], P('dp', 'tensor')
- out_grad: float32 [1152, 1152], P('tensor', 'dp')
- up_grad: float32 [1152, 4304], P('dp', 'tensor')
- down_grad: float32 [4304, 1152], P('tensor', 'dp')
- first_gain_grad: float32 [1152], P('dp')
- first_shift_grad: float32 [1152], P('dp')
- query_bias_grad: float32 [1152], P('dp')
- value_bias_grad: float32 [1152], P('dp')
- out_bias_grad: float32 [1152], P('dp')
- second_gain_grad: float32 [1152], P('dp')
- second_shift_grad: float32 [1152], P('dp')
- up_bias_grad: float32 [4304], P('dp')
- down_bias_grad: float32 [1152], P('dp')
Inputs may be any that keep to these rules, and one draw needn't show every extreme that they name: `key_mask`: each image's ones form a prefix of its positions, at least its first three quarters.
All inputs are finite; a program needn't handle non-finite values.
Results may differ from a plain program's by a relative error of at most 0.017.
The roundings to bfloat16 on the way count: a program that leaves them out, or rounds other values in their place, can miss the bound.
Values may be sent and summed in bfloat16 or wider, within the bound.
A program may use at most 128 MiB of HBM per device.

v0:
```python
from functools import partial
import math
import jax
import jax.numpy as jnp
from jax import lax
from jax.sharding import PartitionSpec as P

HD = 72
EPSILON = 1e-06
GELU_COEF = 0.7978845608028654
MASK_FILL = -1e30


def norm_forward(inputs, gain_vec, shift_vec):
    centred = inputs - jnp.mean(inputs, axis=-1, keepdims=True)
    inv_std = lax.rsqrt(jnp.mean(centred * centred, axis=-1, keepdims=True) + EPSILON)
    normed = centred * inv_std
    return (normed * gain_vec + shift_vec, normed, inv_std)


def norm_backward(grad_in, normed, inv_std, gain_vec):
    scaled = grad_in * gain_vec
    return inv_std * (
        scaled
        - jnp.mean(scaled, axis=-1, keepdims=True)
        - normed * jnp.mean(scaled * normed, axis=-1, keepdims=True)
    )


def gelu_pair(pre_act):
    tanh_val = jnp.tanh(GELU_COEF * (pre_act + 0.044715 * pre_act * pre_act * pre_act))
    gelu_value = 0.5 * pre_act * (1.0 + tanh_val)
    gelu_slope = 0.5 * (1.0 + tanh_val) + 0.5 * pre_act * (
        1.0 - tanh_val * tanh_val
    ) * GELU_COEF * (1.0 + 3.0 * 0.044715 * pre_act * pre_act)
    return (gelu_value, gelu_slope)


def mat_dot(left, right):
    return jnp.dot(left, right, preferred_element_type=jnp.float32)


def gather_rows(local):
    return lax.all_gather(local, "tensor", axis=1, tiled=True)


def sum_rows(partial_term):
    return lax.psum_scatter(
        partial_term.astype(jnp.bfloat16), "tensor", scatter_dimension=1, tiled=True
    ).astype(jnp.float32)


def attend_image(packed):
    query_img, keys_img, values_img, valid_img = packed
    scores = jnp.einsum("qhd,khd->hqk", query_img, keys_img, preferred_element_type=jnp.float32)
    scores = jnp.where(valid_img[None, None, :] > 0, scores, MASK_FILL)
    highest = jnp.max(scores, axis=-1, keepdims=True)
    logsum = highest + jnp.log(jnp.sum(jnp.exp(scores - highest), axis=-1, keepdims=True))
    probs = jnp.exp(scores - logsum).astype(jnp.bfloat16)
    mixed = jnp.einsum("hqk,khd->qhd", probs, values_img, preferred_element_type=jnp.float32)
    return (mixed.astype(jnp.bfloat16), logsum[..., 0])


def attend_back(scale_factor, packed):
    query_img, keys_img, values_img, valid_img, logsum_img, mixed_img, grad_img = packed
    scores = jnp.einsum("qhd,khd->hqk", query_img, keys_img, preferred_element_type=jnp.float32)
    scores = jnp.where(valid_img[None, None, :] > 0, scores, MASK_FILL)
    probs_full = jnp.exp(scores - logsum_img[:, :, None])
    probs = probs_full.astype(jnp.bfloat16)
    grad_values = jnp.einsum("hqk,qhd->khd", probs, grad_img, preferred_element_type=jnp.float32)
    grad_probs = jnp.einsum(
        "qhd,khd->hqk", grad_img, values_img, preferred_element_type=jnp.float32
    )
    delta = jnp.sum(grad_img.astype(jnp.float32) * mixed_img.astype(jnp.float32), axis=-1).T
    grad_scores = (probs_full * (grad_probs - delta[:, :, None])).astype(jnp.bfloat16)
    grad_query = (
        jnp.einsum("hqk,khd->qhd", grad_scores, keys_img, preferred_element_type=jnp.float32)
        * scale_factor
    )
    grad_keys = jnp.einsum(
        "hqk,qhd->khd", grad_scores, query_img, preferred_element_type=jnp.float32
    )
    return (grad_query, grad_keys, grad_values)


def vector_share(full_vec, parts, index):
    piece = full_vec.shape[0] // parts
    return lax.dynamic_slice_in_dim(full_vec, index * piece, piece)


def shards(
    tokens,
    key_mask,
    query_weight,
    key_weight,
    value_weight,
    out_weight,
    up_weight,
    down_weight,
    first_gain,
    first_shift,
    query_bias,
    value_bias,
    out_bias,
    second_gain,
    second_shift,
    up_bias,
    down_bias,
    cotangent,
):
    dp_count = lax.axis_size("dp")
    dp_index = lax.axis_index("dp")
    tensor_index = lax.axis_index("tensor")
    images = tokens.shape[0]
    width = tokens.shape[2]
    fetched = (
        lax.all_gather(query_weight, "dp", axis=0, tiled=True),
        lax.all_gather(key_weight, "dp", axis=0, tiled=True),
        lax.all_gather(value_weight, "dp", axis=0, tiled=True),
        lax.all_gather(out_weight, "dp", axis=1, tiled=True),
        lax.all_gather(up_weight, "dp", axis=0, tiled=True),
        lax.all_gather(down_weight, "dp", axis=1, tiled=True),
        lax.all_gather(first_gain, "dp", axis=0, tiled=True),
        lax.all_gather(first_shift, "dp", axis=0, tiled=True),
        lax.all_gather(query_bias, "dp", axis=0, tiled=True),
        lax.all_gather(value_bias, "dp", axis=0, tiled=True),
        lax.all_gather(out_bias, "dp", axis=0, tiled=True),
        lax.all_gather(second_gain, "dp", axis=0, tiled=True),
        lax.all_gather(second_shift, "dp", axis=0, tiled=True),
        lax.all_gather(up_bias, "dp", axis=0, tiled=True),
        lax.all_gather(down_bias, "dp", axis=0, tiled=True),
    )
    query_full, key_full, value_full, out_full, up_full, down_full = fetched[:6]
    (
        gain_one,
        shift_one,
        query_bias_all,
        value_bias_all,
        out_bias_all,
        gain_two,
        shift_two,
        up_bias_all,
        down_bias_all,
    ) = [member.astype(jnp.float32) for member in fetched[6:]]
    head_cols = query_full.shape[1]
    hidden_cols = up_full.shape[1]
    heads_local = head_cols // HD
    query_bias_local = lax.dynamic_slice_in_dim(query_bias_all, tensor_index * head_cols, head_cols)
    value_bias_local = lax.dynamic_slice_in_dim(value_bias_all, tensor_index * head_cols, head_cols)
    up_bias_local = lax.dynamic_slice_in_dim(up_bias_all, tensor_index * hidden_cols, hidden_cols)
    scale_factor = 1.0 / math.sqrt(HD)
    inputs = tokens.astype(jnp.float32)
    first, normed_one, inv_one = norm_forward(inputs, gain_one, shift_one)
    first_rows = gather_rows(first.astype(jnp.bfloat16))
    seq_full = first_rows.shape[1]
    row_shape = (images, seq_full, width)
    head_shape = (images, seq_full, heads_local, HD)
    first_flat = first_rows.reshape(-1, width)
    query = (
        ((mat_dot(first_flat, query_full) + query_bias_local) * scale_factor)
        .astype(jnp.bfloat16)
        .reshape(head_shape)
    )
    keys = mat_dot(first_flat, key_full).astype(jnp.bfloat16).reshape(head_shape)
    values = (
        (mat_dot(first_flat, value_full) + value_bias_local)
        .astype(jnp.bfloat16)
        .reshape(head_shape)
    )
    mixed, logsum = lax.map(attend_image, (query, keys, values, key_mask))
    mixed_flat = mixed.reshape(-1, head_cols)
    hidden = inputs + sum_rows(mat_dot(mixed_flat, out_full).reshape(row_shape)) + out_bias_all
    second, normed_two, inv_two = norm_forward(hidden, gain_two, shift_two)
    second_flat = gather_rows(second.astype(jnp.bfloat16)).reshape(-1, width)
    pre_act = mat_dot(second_flat, up_full) + up_bias_local
    gelu_value, gelu_slope = gelu_pair(pre_act)
    act = gelu_value.astype(jnp.bfloat16)
    output = (hidden + sum_rows(mat_dot(act, down_full).reshape(row_shape)) + down_bias_all).astype(
        jnp.bfloat16
    )
    query_back, key_back, value_back, out_back, up_back, down_back = (
        lax.all_gather(query_weight, "dp", axis=0, tiled=True),
        lax.all_gather(key_weight, "dp", axis=0, tiled=True),
        lax.all_gather(value_weight, "dp", axis=0, tiled=True),
        lax.all_gather(out_weight, "dp", axis=1, tiled=True),
        lax.all_gather(up_weight, "dp", axis=0, tiled=True),
        lax.all_gather(down_weight, "dp", axis=1, tiled=True),
    )
    grad_out = cotangent.astype(jnp.float32)
    down_bias_grad = jnp.sum(grad_out, axis=(0, 1))
    grad_rows = gather_rows(cotangent).reshape(-1, width)
    down_grad = mat_dot(act.T, grad_rows)
    grad_pre = mat_dot(grad_rows, down_back.T) * gelu_slope
    up_bias_part = jnp.sum(grad_pre, axis=0)
    grad_pre_low = grad_pre.astype(jnp.bfloat16)
    up_grad = mat_dot(second_flat.T, grad_pre_low)
    grad_second = sum_rows(mat_dot(grad_pre_low, up_back.T).reshape(row_shape))
    second_gain_grad = jnp.sum(grad_second * normed_two, axis=(0, 1))
    second_shift_grad = jnp.sum(grad_second, axis=(0, 1))
    grad_hidden = grad_out + norm_backward(grad_second, normed_two, inv_two, gain_two)
    out_bias_grad = jnp.sum(grad_hidden, axis=(0, 1))
    hidden_rows = gather_rows(grad_hidden.astype(jnp.bfloat16)).reshape(-1, width)
    grad_mixed = mat_dot(hidden_rows, out_back.T).astype(jnp.bfloat16)
    out_grad = mat_dot(mixed_flat.T, hidden_rows)
    grad_query_f, grad_keys_f, grad_values_f = lax.map(
        partial(attend_back, scale_factor),
        (query, keys, values, key_mask, logsum, mixed, grad_mixed.reshape(head_shape)),
    )
    grad_query_f = grad_query_f.reshape(-1, head_cols)
    grad_keys_f = grad_keys_f.reshape(-1, head_cols)
    grad_values_f = grad_values_f.reshape(-1, head_cols)
    query_bias_part = jnp.sum(grad_query_f, axis=0)
    value_bias_part = jnp.sum(grad_values_f, axis=0)
    grad_query = grad_query_f.astype(jnp.bfloat16)
    grad_keys = grad_keys_f.astype(jnp.bfloat16)
    grad_values = grad_values_f.astype(jnp.bfloat16)
    query_grad = mat_dot(first_flat.T, grad_query)
    key_grad = mat_dot(first_flat.T, grad_keys)
    value_grad = mat_dot(first_flat.T, grad_values)
    first_term = (
        mat_dot(grad_query, query_back.T)
        + mat_dot(grad_keys, key_back.T)
        + mat_dot(grad_values, value_back.T)
    )
    grad_first = sum_rows(first_term.reshape(row_shape))
    first_gain_grad = jnp.sum(grad_first * normed_one, axis=(0, 1))
    first_shift_grad = jnp.sum(grad_first, axis=(0, 1))
    input_grad = grad_hidden + norm_backward(grad_first, normed_one, inv_one, gain_one)
    matrix_shares = (
        lax.psum_scatter(query_grad, "dp", scatter_dimension=0, tiled=True),
        lax.psum_scatter(key_grad, "dp", scatter_dimension=0, tiled=True),
        lax.psum_scatter(value_grad, "dp", scatter_dimension=0, tiled=True),
        lax.psum_scatter(out_grad, "dp", scatter_dimension=1, tiled=True),
        lax.psum_scatter(up_grad, "dp", scatter_dimension=0, tiled=True),
        lax.psum_scatter(down_grad, "dp", scatter_dimension=1, tiled=True),
    )
    query_bias_full = lax.dynamic_update_slice_in_dim(
        jnp.zeros((width,), jnp.float32), query_bias_part, tensor_index * head_cols, 0
    )
    value_bias_full = lax.dynamic_update_slice_in_dim(
        jnp.zeros((width,), jnp.float32), value_bias_part, tensor_index * head_cols, 0
    )
    up_bias_full = lax.dynamic_update_slice_in_dim(
        jnp.zeros((up_bias_all.shape[0],), jnp.float32), up_bias_part, tensor_index * hidden_cols, 0
    )
    vector_sums = lax.psum(
        (
            first_gain_grad,
            first_shift_grad,
            query_bias_full,
            value_bias_full,
            out_bias_grad,
            second_gain_grad,
            second_shift_grad,
            up_bias_full,
            down_bias_grad,
        ),
        ("dp", "tensor"),
    )
    vector_parts = tuple((vector_share(member, dp_count, dp_index) for member in vector_sums))
    return (output, input_grad) + tuple(matrix_shares) + vector_parts


def solution(mesh):
    return jax.shard_map(
        shards,
        mesh=mesh,
        in_specs=(
            P("dp", "tensor", None),
            P("dp", None),
            P("dp", "tensor"),
            P("dp", "tensor"),
            P("dp", "tensor"),
            P("tensor", "dp"),
            P("dp", "tensor"),
            P("tensor", "dp"),
            P("dp"),
            P("dp"),
            P("dp"),
            P("dp"),
            P("dp"),
            P("dp"),
            P("dp"),
            P("dp"),
            P("dp"),
            P("dp", "tensor", None),
        ),
        out_specs=(
            P("dp", "tensor", None),
            P("dp", "tensor", None),
            P("dp", "tensor"),
            P("dp", "tensor"),
            P("dp", "tensor"),
            P("tensor", "dp"),
            P("dp", "tensor"),
            P("tensor", "dp"),
            P("dp"),
            P("dp"),
            P("dp"),
            P("dp"),
            P("dp"),
            P("dp"),
            P("dp"),
            P("dp"),
            P("dp"),
        ),
        check_vma=False,
    )
```

profile of v0, /device:TPU:0, one launch (start us, length us, event | category | flops | bytes accessed | tf_op | source)
XLA Modules:
  0.0 748.6 jit_solution(14068338893583376241)
XLA Ops:
  20.8 26.1 %all-reduce.14 = (bf16[1152]{0:T(1024)(128)(2,1)S(1)}, bf16[1152]{0:T(1024)(128)(2,1)S(1)}, bf16[1152]{0:T(1024)(128)(2,1)S(1)}, bf16[1152]{0:T(1024)(128)(2,1)S...) all-reduce(bf16[1152]{0:T(1024)(128)(2,1)S(1)} %dynamic-update-slic, ...), channel_id=1, replica_groups=mesh['dp'=8,'tensor'=4] {'dp'}, use_global_device_ids=true, to_apply=%add.6 | all-reduce | flops 13520 | bytes 54080
  49.9 10.0 %all_gather.68 = bf16[1152,288]{1,0:T(8,128)(2,1)S(1)} all-gather(bf16[144,288]{1,0:T(8,128)(2,1)} %param.20), channel_id=1, replica_groups=mesh['dp'=8,'tensor'=4] {'dp'}, dimensions={0}, use_global_device_ids=true | all-gather | bytes 746496 | tf_op jit(solution)/shard_map/all_gather | solution.py:117
  59.9 10.5 %all_gather.70 = bf16[1152,288]{1,0:T(8,128)(2,1)S(1)} all-gather(bf16[144,288]{1,0:T(8,128)(2,1)S(1)} %copy-done.18), channel_id=1, replica_groups=mesh['dp'=8,'tensor'=4] {'dp'}, dimensions={0}, use_global_device_ids=true | all-gather | bytes 746496 | tf_op jit(solution)/shard_map/all_gather | solution.py:118
  70.4 10.2 %all_gather.66 = bf16[1152,288]{1,0:T(8,128)(2,1)S(1)} all-gather(bf16[144,288]{1,0:T(8,128)(2,1)S(1)} %copy-done.19), channel_id=1, replica_groups=mesh['dp'=8,'tensor'=4] {'dp'}, dimensions={0}, use_global_device_ids=true | all-gather | bytes 746496 | tf_op jit(solution)/shard_map/all_gather | solution.py:119
  80.5 11.5 %all_gather.71 = bf16[288,1152]{0,1:T(8,128)(2,1)} all-gather(bf16[288,144]{0,1:T(8,128)(2,1)S(1)} %copy-done.20), channel_id=1, replica_groups=mesh['dp'=8,'tensor'=4] {'dp'}, dimensions={1}, use_global_device_ids=true | all-gather | bytes 746496 | tf_op jit(solution)/shard_map/all_gather | solution.py:120
  106.2 37.0 %reduce-scatter.35.cloned.1.call-done = bf16[1,184,1152]{2,1,0:T(8,128)(2,1)} async-done(((bf16[1,736,1152]{2,1,0:T(8,128)(2,1)}), bf16[1,184,1152]{2,1,0:T(8,128)(2,1)}) %reduce-scatter.35.cloned.1.call-update) | async-done | bytes 423952
  149.5 36.8 %all-gather.9.cloned.1.call-done = bf16[1,736,1152]{2,1,0:T(8,128)(2,1)} async-done(((bf16[1,184,1152]{2,1,0:T(8,128)(2,1)}), bf16[1,736,1152]{2,1,0:T(8,128)(2,1)}) %all-gather.9.cloned.1.call-update) | async-done | bytes 1695760 | tf_op jit(solution)/shard_map/all_gather | solution.py:44
  186.3 6.4 convolution_add_fusion.2
  192.8 32.8 %all-gather.15.cloned.1.call-done = bf16[1,736,1152]{2,1,0:T(8,128)(2,1)} async-done(((bf16[1,184,1152]{2,1,0:T(8,128)(2,1)}), bf16[1,736,1152]{2,1,0:T(8,128)(2,1)}) %all-gather.15.cloned.1.call-update) | async-done | bytes 1695760 | tf_op jit(solution)/shard_map/all_gather | solution.py:44
  225.6 30.9 %all-gather.13.cloned.1.call-done = bf16[1076,1152]{0,1:T(8,128)(2,1)} async-done(((bf16[1076,144]{0,1:T(8,128)(2,1)}), bf16[1076,1152]{0,1:T(8,128)(2,1)}) %all-gather.13.cloned.1.call-update) | async-done | bytes 2479120 | tf_op jit(solution)/shard_map/all_gather | solution.py:122
  256.5 8.2 %fusion.86 = (f32[1076]{0:T(1024)}, bf16[736,1076]{0,1:T(8,128)(2,1)S(1)}) fusion(f32[736,1076]{0,1:T(8,128)} %convolution_add_fusion.2, bf16[1076,1152]{0,1:T(8,128)(2,1)} %all-gather.13.cloned.1.call-done, bf16[1,736,1152]{2,1,0:T(8,128)(2,1)} %all-gather.15.cloned.1.call-done), kind=kOutput, calls=%fused_computation.117 | convolution fusion | flops 1840458240 | bytes 8930768 | tf_op jit(solution)/shard_map/dot_general | solution.py:40
  265.9 4.0 fusion.8
  269.9 7.2 fusion.7
  277.2 30.1 %reduce-scatter.39.cloned.1.call-done = bf16[1,184,1152]{2,1,0:T(8,128)(2,1)} async-done(((bf16[1,736,1152]{2,1,0:T(8,128)(2,1)}), bf16[1,184,1152]{2,1,0:T(8,128)(2,1)}) %reduce-scatter.39.cloned.1.call-update) | async-done | bytes 423952
  309.5 36.8 %reduce-scatter.37.cloned.1.call-done = bf16[1,184,1152]{2,1,0:T(8,128)(2,1)} async-done(((bf16[1,736,1152]{2,1,0:T(8,128)(2,1)}), bf16[1,184,1152]{2,1,0:T(8,128)(2,1)}) %reduce-scatter.37.cloned.1.call-update) | async-done | bytes 423952
  350.3 38.2 %all-gather.17.cloned.1.call-done = bf16[1,736,1152]{2,1,0:T(8,128)(2,1)} async-done(((bf16[1,184,1152]{2,1,0:T(8,128)(2,1)}), bf16[1,736,1152]{2,1,0:T(8,128)(2,1)}) %all-gather.17.cloned.1.call-update) | async-done | bytes 1695760 | tf_op jit(solution)/shard_map/all_gather | solution.py:44
  392.1 5.6 fusion.84
  397.8 5.6 multiply_convert_fusion
  410.8 7.4 fusion.15
  419.7 6.5 fusion.18
  427.2 3.9 fusion.11
  431.2 3.9 fusion.21
  435.2 3.9 fusion.25
  439.2 3.8 fusion.23
  444.0 2.7 reduce-scatter.41.cloned.1.call-done
  448.2 41.8 %all-reduce.13 = (f32[1152]{0:T(1024)S(1)}, f32[1152]{0:T(1024)S(1)}, f32[1152]{0:T(1024)S(1)}, f32[1152]{0:T(1024)S(1)}, f32[1152]{0:T(1024)S(1)}, /*index=5*/f...) all-reduce(f32[1152]{0:T(1024)S(1)} %get-tuple-element.73, ...), channel_id=1, replica_groups=mesh['dp'=8,'tensor'=4] {'dp','tensor'}, use_global_device_ids=true, to_apply=%region_22.23 | all-reduce | flops 13520 | bytes 108160 | tf_op jit(solution)/shard_map/psum | solution.py:246
  498.0 9.4 %reduce-scatter.33.cloned.1.call-done = f32[1076,144]{0,1:T(8,128)} async-done(((f32[1076,1152]{0,1:T(8,128)}), f32[1076,144]{0,1:T(8,128)}) %reduce-scatter.33.cloned.1.call-update) | async-done | bytes 619792 | tf_op jit(solution)/shard_map/reduce_scatter | solution.py:235
  507.5 61.1 %reduce-scatter.31.cloned.1.call-done = f32[144,1076]{1,0:T(8,128)} async-done(((f32[1152,1076]{1,0:T(8,128)}), f32[144,1076]{1,0:T(8,128)}) %reduce-scatter.31.cloned.1.call-update) | async-done | bytes 619792 | tf_op jit(solution)/shard_map/reduce_scatter | solution.py:234
  568.5 43.1 %reduce-scatter.29.cloned.1.call-done = f32[288,144]{0,1:T(8,128)} async-done(((f32[288,1152]{0,1:T(8,128)}), f32[288,144]{0,1:T(8,128)}) %reduce-scatter.29.cloned.1.call-update) | async-done | bytes 165904 | tf_op jit(solution)/shard_map/reduce_scatter | solution.py:233
  611.6 43.1 %reduce-scatter.27.cloned.1.call-done = f32[144,288]{1,0:T(8,128)} async-done(((f32[1152,288]{1,0:T(8,128)}), f32[144,288]{1,0:T(8,128)}) %reduce-scatter.27.cloned.1.call-update) | async-done | bytes 165904 | tf_op jit(solution)/shard_map/reduce_scatter | solution.py:232
  654.7 43.3 %reduce-scatter.23.cloned.1.call-done = f32[144,288]{1,0:T(8,128)} async-done(((f32[1152,288]{1,0:T(8,128)}), f32[144,288]{1,0:T(8,128)}) %reduce-scatter.23.cloned.1.call-update) | async-done | bytes 165904 | tf_op jit(solution)/shard_map/reduce_scatter | solution.py:230
  698.0 43.1 %reduce-scatter.25.cloned.1.call-done = f32[144,288]{1,0:T(8,128)} async-done(((f32[1152,288]{1,0:T(8,128)}), f32[144,288]{1,0:T(8,128)}) %reduce-scatter.25.cloned.1.call-update) | async-done | bytes 165904 | tf_op jit(solution)/shard_map/reduce_scatter | solution.py:231
  (173 shorter events, 66.2 us)
Async XLA Ops:
  8.0 51.8 %copy-start.18 = (bf16[144,288]{1,0:T(8,128)(2,1)S(1)}, bf16[144,288]{1,0:T(8,128)(2,1)}, u32[]{:S(2)}) copy-start(bf16[144,288]{1,0:T(8,128)(2,1)} %param.21) | copy-start | bytes 248836
  8.0 62.3 %copy-start.19 = (bf16[144,288]{1,0:T(8,128)(2,1)S(1)}, bf16[144,288]{1,0:T(8,128)(2,1)}, u32[]{:S(2)}) copy-start(bf16[144,288]{1,0:T(8,128)(2,1)} %param.22) | copy-start | bytes 248836
  8.0 72.5 %copy-start.20 = (bf16[288,144]{0,1:T(8,128)(2,1)S(1)}, bf16[288,144]{0,1:T(8,128)(2,1)}, u32[]{:S(2)}) copy-start(bf16[288,144]{0,1:T(8,128)(2,1)} %param.23) | copy-start | bytes 248836
  8.1 84.0 %all-gather.7.cloned.1.call-start = ((), (), s32[]{:S(2)}) async-start(), calls=%async_computation.10 | async-start | bytes 2119680 | tf_op jit(solution)/shard_map/all_gather | solution.py:44
  48.9 94.3 %reduce-scatter.35.cloned.1.call-start = ((), (), s32[]{:S(2)}) async-start(), calls=%async_computation.22 | async-start | bytes 2119680
  70.4 24.9 %copy-start.3 = (bf16[1152,288]{1,0:T(8,128)(2,1)}, bf16[1152,288]{1,0:T(8,128)(2,1)S(1)}, u32[]{:S(2)}) copy-start(bf16[1152,288]{1,0:T(8,128)(2,1)S(1)} %all_gather.70) | copy-start | bytes 1990660
  98.8 3.5 copy-start.21
  102.3 40.9 %copy-start = (bf16[1,184,1152]{2,1,0:T(8,128)(2,1)S(1)}, bf16[1,184,1152]{2,1,0:T(8,128)(2,1)}, u32[]{:S(2)}) copy-start(bf16[1,184,1152]{2,1,0:T(8,128)(2,1)} %param.18) | copy-start | bytes 1271812
  105.5 44.0 %all-gather.11.cloned.1.call-start = ((), (), s32[]{:S(2)}) async-start(), calls=%async_computation.12 | async-start | bytes 2985984 | tf_op jit(solution)/shard_map/all_gather | solution.py:121
  106.1 80.2 %all-gather.9.cloned.1.call-start = ((), (), s32[]{:S(2)}) async-start(), calls=%async_computation.11 | async-start | bytes 2119680 | tf_op jit(solution)/shard_map/all_gather | solution.py:44
  147.8 77.8 %all-gather.15.cloned.1.call-start = ((), (), s32[]{:S(2)}) async-start(), calls=%async_computation.14 | async-start | bytes 2119680 | tf_op jit(solution)/shard_map/all_gather | solution.py:44
  148.4 108.1 %all-gather.13.cloned.1.call-start = ((), (), s32[]{:S(2)}) async-start(), calls=%async_computation.13 | async-start | bytes 2985984 | tf_op jit(solution)/shard_map/all_gather | solution.py:122
  149.1 158.2 %reduce-scatter.39.cloned.1.call-start = ((), (), s32[]{:S(2)}) async-start(), calls=%async_computation.24 | async-start | bytes 2119680
  256.5 9.4 %copy-start.24 = (bf16[1152,1076]{1,0:T(8,128)(2,1)S(1)}, bf16[1152,1076]{1,0:T(8,128)(2,1)}, u32[]{:S(2)}) copy-start(bf16[1152,1076]{1,0:T(8,128)(2,1)} %all-gather.11.cloned.1.call-done) | copy-start | bytes 7437316
  269.9 37.4 %copy-start.2 = (bf16[1,184,1152]{2,1,0:T(8,128)(2,1)S(1)}, bf16[1,184,1152]{2,1,0:T(8,128)(2,1)}, u32[]{:S(2)}) copy-start(bf16[1,184,1152]{2,1,0:T(8,128)(2,1)} %reduce-scatter.35.cloned.1.call-done) | copy-start | bytes 1271812
  269.9 76.4 %reduce-scatter.37.cloned.1.call-start = ((), (), s32[]{:S(2)}) async-start(), calls=%async_computation.23 | async-start | bytes 2119680
  277.2 111.3 %all-gather.17.cloned.1.call-start = ((), (), s32[]{:S(2)}) async-start(), calls=%async_computation.15 | async-start | bytes 2119680 | tf_op jit(solution)/shard_map/all_gather | solution.py:44
  348.9 43.2 %copy-start.22 = (f32[4,736]{1,0:T(4,128)S(1)}, f32[4,736]{1,0:T(4,128)}, u32[]{:S(2)}) copy-start(f32[4,736]{1,0:T(4,128)} %copy-done.21) | copy-start | bytes 35332
  349.8 96.9 %reduce-scatter.41.cloned.1.call-start = ((), (), s32[]{:S(2)}) async-start(), calls=%async_computation.25 | async-start | bytes 2119680
  392.1 5.7 copy-start.28
  397.8 10.6 %copy-start.14 = (bf16[736,4,72]{0,2,1:T(8,128)(2,1)}, bf16[736,4,72]{0,2,1:T(8,128)(2,1)S(1)}, u32[]{:S(2)}) copy-start(bf16[736,4,72]{0,2,1:T(8,128)(2,1)S(1)} %get-tuple-element.100) | copy-start | bytes 1271812
  397.8 5.6 copy-start.10
  410.8 96.7 %reduce-scatter.33.cloned.1.call-start = ((), (), s32[]{:S(2)}) async-start(), calls=%async_computation.21 | async-start | bytes 5971968 | tf_op jit(solution)/shard_map/reduce_scatter | solution.py:235
  418.2 150.3 %reduce-scatter.31.cloned.1.call-start = ((), (), s32[]{:S(2)}) async-start(), calls=%async_computation.20 | async-start | bytes 5971968 | tf_op jit(solution)/shard_map/reduce_scatter | solution.py:234
  426.2 5.0 copy-start.15
  426.2 185.4 %reduce-scatter.29.cloned.1.call-start = ((), (), s32[]{:S(2)}) async-start(), calls=%async_computation.19 | async-start | bytes 1990656 | tf_op jit(solution)/shard_map/reduce_scatter | solution.py:233
  431.1 4.1 copy-start.6
  431.1 223.6 %reduce-scatter.27.cloned.1.call-start = ((), (), s32[]{:S(2)}) async-start(), calls=%async_computation.18 | async-start | bytes 1990656 | tf_op jit(solution)/shard_map/reduce_scatter | solution.py:232
  435.1 4.1 copy-start.12
  435.1 262.8 %reduce-scatter.23.cloned.1.call-start = ((), (), s32[]{:S(2)}) async-start(), calls=%async_computation.16 | async-start | bytes 1990656 | tf_op jit(solution)/shard_map/reduce_scatter | solution.py:230
  439.1 3.9 copy-start.23
  439.1 302.0 %reduce-scatter.25.cloned.1.call-start = ((), (), s32[]{:S(2)}) async-start(), calls=%async_computation.17 | async-start | bytes 1990656 | tf_op jit(solution)/shard_map/reduce_scatter | solution.py:231
  (14 other events, 26.0 us)
Sparse Core Ops, SparseCore 0:
  49.1 38.4 all-gather.6
  105.7 37.5 reduce-scatter.34
  270.0 37.2 reduce-scatter.38
  309.5 36.7 reduce-scatter.36
  349.9 38.5 all-gather.16
Sparse Core Ops, SparseCore 1:
  107.9 30.3 all-gather.10
  147.9 38.4 all-gather.8
  187.8 37.8 all-gather.14
  227.5 28.9 all-gather.12
  410.9 35.8 reduce-scatter.40
  450.7 56.7 reduce-scatter.32
  511.7 56.8 reduce-scatter.30
  572.3 39.2 reduce-scatter.28
  615.4 39.2 reduce-scatter.26
  658.7 39.2 reduce-scatter.22
  701.8 39.2 reduce-scatter.24
where the time goes:
time: 754 us; the launch traced here: 749 us
  waiting for transfers between devices  490 us (65%)
  blocking collectives  110 us (15%)
  matrix products  86 us (11%)
  other arithmetic  22.3 us (3%)
  local copies, waits for them, and re-layouts  20.8 us (3%)
  between operations  17.6 us (2%)
    unnamed x20, waiting for transfers between devices  109 us
    all_gather x4, waiting for transfers between devices, gather_rows(): return lax.all_gather(local, 'tensor', axis=1, tiled=True)  108 us
    dot_general x18, matrix products, mat_dot(): return jnp.dot(left, right, preferred_element_type=jnp.float32)  68.7 us
    reduce_scatter x1, waiting for transfers between devices, shards(): lax.psum_scatter(up_grad, 'dp', scatter_dimension=0, tiled=True)  61.1 us
    reduce_scatter x1, waiting for transfers between devices, shards(): lax.psum_scatter(query_grad, 'dp', scatter_dimension=0, tiled=True)  43.3 us
    reduce_scatter x1, waiting for transfers between devices, shards(): lax.psum_scatter(key_grad, 'dp', scatter_dimension=0, tiled=True)  43.1 us
    reduce_scatter x1, waiting for transfers between devices, shards(): lax.psum_scatter(value_grad, 'dp', scatter_dimension=0, tiled=True)  43.1 us
    reduce_scatter x1, waiting for transfers between devices, shards(): lax.psum_scatter(out_grad, 'dp', scatter_dimension=1, tiled=True)  43.1 us
  transfers between devices with their start and end apart: 16, of which 14 were waited for; matrix products, arithmetic and copies ran while one was open for 8% of the time, Pallas kernels for 0%

commit v1 on v0

--- a/solution.py
+++ b/solution.py
@@ -244,18 +244,21 @@
         jnp.zeros((up_bias_all.shape[0],), jnp.float32), up_bias_part, tensor_index * hidden_cols, 0
     )
     vector_sums = lax.psum(
-        (
-            first_gain_grad,
-            first_shift_grad,
-            query_bias_full,
-            value_bias_full,
-            out_bias_grad,
-            second_gain_grad,
-            second_shift_grad,
-            up_bias_full,
-            down_bias_grad,
+        lax.psum(
+            (
+                first_gain_grad,
+                first_shift_grad,
+                query_bias_full,
+                value_bias_full,
+                out_bias_grad,
+                second_gain_grad,
+                second_shift_grad,
+                up_bias_full,
+                down_bias_grad,
+            ),
+            "tensor",
         ),
-        ("dp", "tensor"),
+        "dp",
     )
     vector_parts = tuple((vector_share(member, dp_count, dp_index) for member in vector_sums))
     return (output, input_grad) + tuple(matrix_shares) + vector_parts

time: 754 us -> 754 us (level)
    psum x0 -> x1, blocking collectives: none -> 24.7 us  [shards(): lax.psum(lax.psum((first_gain_grad, first_shift_grad, query_bias_full, va...]
    psum x1, blocking collectives: 41.8 us -> 18.7 us  [shards(): lax.psum((first_gain_grad, first_shift_grad, query_bias_full, value_bias_...]
where the time goes in v1:
time: 754 us; the launch traced here: 749 us
  waiting for transfers between devices  489 us (65%)
  blocking collectives  112 us (15%)
  matrix products  86 us (11%)
  other arithmetic  22.3 us (3%)
  local copies, waits for them, and re-layouts  20.8 us (3%)
  between operations  17.6 us (2%)
    unnamed x20, waiting for transfers between devices  109 us
    all_gather x4, waiting for transfers between devices, gather_rows(): return lax.all_gather(local, 'tensor', axis=1, tiled=True)  108 us
    dot_general x18, matrix products, mat_dot(): return jnp.dot(left, right, preferred_element_type=jnp.float32)  68.7 us
    reduce_scatter x1, waiting for transfers between devices, shards(): lax.psum_scatter(up_grad, 'dp', scatter_dimension=0, tiled=True)  61 us
    reduce_scatter x1, waiting for transfers between devices, shards(): lax.psum_scatter(query_grad, 'dp', scatter_dimension=0, tiled=True)  43.3 us
    reduce_scatter x1, waiting for transfers between devices, shards(): lax.psum_scatter(value_grad, 'dp', scatter_dimension=0, tiled=True)  43.1 us
    reduce_scatter x1, waiting for transfers between devices, shards(): lax.psum_scatter(key_grad, 'dp', scatter_dimension=0, tiled=True)  43.1 us
    reduce_scatter x1, waiting for transfers between devices, shards(): lax.psum_scatter(out_grad, 'dp', scatter_dimension=1, tiled=True)  43.1 us
  transfers between devices with their start and end apart: 16, of which 14 were waited for; matrix products, arithmetic and copies ran while one was open for 8% of the time, Pallas kernels for 0%

profile of v1, /device:TPU:0, one launch (start us, length us, event | category | flops | bytes accessed | tf_op | source)
XLA Modules:
  0.0 748.9 jit_solution(6385166101310155519)
XLA Ops:
  20.8 26.1 %all-reduce.15 = (bf16[1152]{0:T(1024)(128)(2,1)S(1)}, bf16[1152]{0:T(1024)(128)(2,1)S(1)}, bf16[1152]{0:T(1024)(128)(2,1)S(1)}, bf16[1152]{0:T(1024)(128)(2,1)S...) all-reduce(bf16[1152]{0:T(1024)(128)(2,1)S(1)} %dynamic-update-slic, ...), channel_id=1, replica_groups=mesh['dp'=8,'tensor'=4] {'dp'}, use_global_device_ids=true, to_apply=%add.6 | all-reduce | flops 13520 | bytes 54080
  49.9 10.0 %all_gather.68 = bf16[1152,288]{1,0:T(8,128)(2,1)S(1)} all-gather(bf16[144,288]{1,0:T(8,128)(2,1)} %param.20), channel_id=1, replica_groups=mesh['dp'=8,'tensor'=4] {'dp'}, dimensions={0}, use_global_device_ids=true | all-gather | bytes 746496 | tf_op jit(solution)/shard_map/all_gather | solution.py:117
  59.9 10.5 %all_gather.70 = bf16[1152,288]{1,0:T(8,128)(2,1)S(1)} all-gather(bf16[144,288]{1,0:T(8,128)(2,1)S(1)} %copy-done.18), channel_id=1, replica_groups=mesh['dp'=8,'tensor'=4] {'dp'}, dimensions={0}, use_global_device_ids=true | all-gather | bytes 746496 | tf_op jit(solution)/shard_map/all_gather | solution.py:118
  70.4 10.2 %all_gather.66 = bf16[1152,288]{1,0:T(8,128)(2,1)S(1)} all-gather(bf16[144,288]{1,0:T(8,128)(2,1)S(1)} %copy-done.19), channel_id=1, replica_groups=mesh['dp'=8,'tensor'=4] {'dp'}, dimensions={0}, use_global_device_ids=true | all-gather | bytes 746496 | tf_op jit(solution)/shard_map/all_gather | solution.py:119
  80.5 11.5 %all_gather.71 = bf16[288,1152]{0,1:T(8,128)(2,1)} all-gather(bf16[288,144]{0,1:T(8,128)(2,1)S(1)} %copy-done.20), channel_id=1, replica_groups=mesh['dp'=8,'tensor'=4] {'dp'}, dimensions={1}, use_global_device_ids=true | all-gather | bytes 746496 | tf_op jit(solution)/shard_map/all_gather | solution.py:120
  106.2 37.0 %reduce-scatter.35.cloned.1.call-done = bf16[1,184,1152]{2,1,0:T(8,128)(2,1)} async-done(((bf16[1,736,1152]{2,1,0:T(8,128)(2,1)}), bf16[1,184,1152]{2,1,0:T(8,128)(2,1)}) %reduce-scatter.35.cloned.1.call-update) | async-done | bytes 423952
  149.5 36.8 %all-gather.9.cloned.1.call-done = bf16[1,736,1152]{2,1,0:T(8,128)(2,1)} async-done(((bf16[1,184,1152]{2,1,0:T(8,128)(2,1)}), bf16[1,736,1152]{2,1,0:T(8,128)(2,1)}) %all-gather.9.cloned.1.call-update) | async-done | bytes 1695760 | tf_op jit(solution)/shard_map/all_gather | solution.py:44
  186.3 6.4 convolution_add_fusion.2
  192.8 32.8 %all-gather.15.cloned.1.call-done = bf16[1,736,1152]{2,1,0:T(8,128)(2,1)} async-done(((bf16[1,184,1152]{2,1,0:T(8,128)(2,1)}), bf16[1,736,1152]{2,1,0:T(8,128)(2,1)}) %all-gather.15.cloned.1.call-update) | async-done | bytes 1695760 | tf_op jit(solution)/shard_map/all_gather | solution.py:44
  225.6 30.9 %all-gather.13.cloned.1.call-done = bf16[1076,1152]{0,1:T(8,128)(2,1)} async-done(((bf16[1076,144]{0,1:T(8,128)(2,1)}), bf16[1076,1152]{0,1:T(8,128)(2,1)}) %all-gather.13.cloned.1.call-update) | async-done | bytes 2479120 | tf_op jit(solution)/shard_map/all_gather | solution.py:122
  256.5 8.2 %fusion.86 = (f32[1076]{0:T(1024)}, bf16[736,1076]{0,1:T(8,128)(2,1)S(1)}) fusion(f32[736,1076]{0,1:T(8,128)} %convolution_add_fusion.2, bf16[1076,1152]{0,1:T(8,128)(2,1)} %all-gather.13.cloned.1.call-done, bf16[1,736,1152]{2,1,0:T(8,128)(2,1)} %all-gather.15.cloned.1.call-done), kind=kOutput, calls=%fused_computation.117 | convolution fusion | flops 1840458240 | bytes 8930768 | tf_op jit(solution)/shard_map/dot_general | solution.py:40
  265.9 4.0 fusion.8
  269.9 7.2 fusion.7
  277.2 30.1 %reduce-scatter.39.cloned.1.call-done = bf16[1,184,1152]{2,1,0:T(8,128)(2,1)} async-done(((bf16[1,736,1152]{2,1,0:T(8,128)(2,1)}), bf16[1,184,1152]{2,1,0:T(8,128)(2,1)}) %reduce-scatter.39.cloned.1.call-update) | async-done | bytes 423952
  309.5 36.8 %reduce-scatter.37.cloned.1.call-done = bf16[1,184,1152]{2,1,0:T(8,128)(2,1)} async-done(((bf16[1,736,1152]{2,1,0:T(8,128)(2,1)}), bf16[1,184,1152]{2,1,0:T(8,128)(2,1)}) %reduce-scatter.37.cloned.1.call-update) | async-done | bytes 423952
  350.2 38.2 %all-gather.17.cloned.1.call-done = bf16[1,736,1152]{2,1,0:T(8,128)(2,1)} async-done(((bf16[1,184,1152]{2,1,0:T(8,128)(2,1)}), bf16[1,736,1152]{2,1,0:T(8,128)(2,1)}) %all-gather.17.cloned.1.call-update) | async-done | bytes 1695760 | tf_op jit(solution)/shard_map/all_gather | solution.py:44
  392.1 5.6 fusion.84
  397.8 5.6 multiply_convert_fusion
  410.8 7.4 fusion.15
  419.7 6.5 fusion.18
  427.2 3.9 fusion.11
  431.2 3.9 fusion.21
  435.2 3.9 fusion.25
  439.2 3.8 fusion.23
  448.2 18.7 %all-reduce.14 = (f32[1152]{0:T(1024)S(1)}, f32[1152]{0:T(1024)S(1)}, f32[1152]{0:T(1024)S(1)}, f32[1152]{0:T(1024)S(1)}, f32[1152]{0:T(1024)S(1)}, /*index=5*/f...) all-reduce(f32[1152]{0:T(1024)S(1)} %get-tuple-element.73, ...), channel_id=1, replica_groups=mesh['dp'=8,'tensor'=4] {'tensor'}, use_global_device_ids=true, to_apply=%region_22.23 | all-reduce | flops 13520 | bytes 108160 | tf_op jit(solution)/shard_map/psum | solution.py:247
  466.9 24.7 %all-reduce.13 = (f32[1152]{0:T(1024)S(1)}, f32[1152]{0:T(1024)S(1)}, f32[1152]{0:T(1024)S(1)}, f32[1152]{0:T(1024)S(1)}, f32[1152]{0:T(1024)S(1)}, /*index=5*/f...) all-reduce(f32[1152]{0:T(1024)S(1)} %get-tuple-element.88, ...), channel_id=1, replica_groups=mesh['dp'=8,'tensor'=4] {'dp'}, use_global_device_ids=true, to_apply=%region_23.24 | all-reduce | flops 13520 | bytes 108160 | tf_op jit(solution)/shard_map/psum | solution.py:246
  499.6 8.2 %reduce-scatter.33.cloned.1.call-done = f32[1076,144]{0,1:T(8,128)} async-done(((f32[1076,1152]{0,1:T(8,128)}), f32[1076,144]{0,1:T(8,128)}) %reduce-scatter.33.cloned.1.call-update) | async-done | bytes 619792 | tf_op jit(solution)/shard_map/reduce_scatter | solution.py:235
  507.8 61.0 %reduce-scatter.31.cloned.1.call-done = f32[144,1076]{1,0:T(8,128)} async-done(((f32[1152,1076]{1,0:T(8,128)}), f32[144,1076]{1,0:T(8,128)}) %reduce-scatter.31.cloned.1.call-update) | async-done | bytes 619792 | tf_op jit(solution)/shard_map/reduce_scatter | solution.py:234
  568.8 43.1 %reduce-scatter.29.cloned.1.call-done = f32[288,144]{0,1:T(8,128)} async-done(((f32[288,1152]{0,1:T(8,128)}), f32[288,144]{0,1:T(8,128)}) %reduce-scatter.29.cloned.1.call-update) | async-done | bytes 165904 | tf_op jit(solution)/shard_map/reduce_scatter | solution.py:233
  611.9 43.1 %reduce-scatter.27.cloned.1.call-done = f32[144,288]{1,0:T(8,128)} async-done(((f32[1152,288]{1,0:T(8,128)}), f32[144,288]{1,0:T(8,128)}) %reduce-scatter.27.cloned.1.call-update) | async-done | bytes 165904 | tf_op jit(solution)/shard_map/reduce_scatter | solution.py:232
  655.0 43.3 %reduce-scatter.23.cloned.1.call-done = f32[144,288]{1,0:T(8,128)} async-done(((f32[1152,288]{1,0:T(8,128)}), f32[144,288]{1,0:T(8,128)}) %reduce-scatter.23.cloned.1.call-update) | async-done | bytes 165904 | tf_op jit(solution)/shard_map/reduce_scatter | solution.py:230
  698.3 43.1 %reduce-scatter.25.cloned.1.call-done = f32[144,288]{1,0:T(8,128)} async-done(((f32[1152,288]{1,0:T(8,128)}), f32[144,288]{1,0:T(8,128)}) %reduce-scatter.25.cloned.1.call-update) | async-done | bytes 165904 | tf_op jit(solution)/shard_map/reduce_scatter | solution.py:231
  (174 shorter events, 68.8 us)
Async XLA Ops:
  8.0 51.8 %copy-start.18 = (bf16[144,288]{1,0:T(8,128)(2,1)S(1)}, bf16[144,288]{1,0:T(8,128)(2,1)}, u32[]{:S(2)}) copy-start(bf16[144,288]{1,0:T(8,128)(2,1)} %param.21) | copy-start | bytes 248836
  8.0 62.3 %copy-start.19 = (bf16[144,288]{1,0:T(8,128)(2,1)S(1)}, bf16[144,288]{1,0:T(8,128)(2,1)}, u32[]{:S(2)}) copy-start(bf16[144,288]{1,0:T(8,128)(2,1)} %param.22) | copy-start | bytes 248836
  8.0 72.5 %copy-start.20 = (bf16[288,144]{0,1:T(8,128)(2,1)S(1)}, bf16[288,144]{0,1:T(8,128)(2,1)}, u32[]{:S(2)}) copy-start(bf16[288,144]{0,1:T(8,128)(2,1)} %param.23) | copy-start | bytes 248836
  8.1 84.0 %all-gather.7.cloned.1.call-start = ((), (), s32[]{:S(2)}) async-start(), calls=%async_computation.10 | async-start | bytes 2119680 | tf_op jit(solution)/shard_map/all_gather | solution.py:44
  48.9 94.3 %reduce-scatter.35.cloned.1.call-start = ((), (), s32[]{:S(2)}) async-start(), calls=%async_computation.22 | async-start | bytes 2119680
  70.4 24.9 %copy-start.3 = (bf16[1152,288]{1,0:T(8,128)(2,1)}, bf16[1152,288]{1,0:T(8,128)(2,1)S(1)}, u32[]{:S(2)}) copy-start(bf16[1152,288]{1,0:T(8,128)(2,1)S(1)} %all_gather.70) | copy-start | bytes 1990660
  98.8 3.5 copy-start.21
  102.3 40.9 %copy-start = (bf16[1,184,1152]{2,1,0:T(8,128)(2,1)S(1)}, bf16[1,184,1152]{2,1,0:T(8,128)(2,1)}, u32[]{:S(2)}) copy-start(bf16[1,184,1152]{2,1,0:T(8,128)(2,1)} %param.18) | copy-start | bytes 1271812
  105.5 44.0 %all-gather.11.cloned.1.call-start = ((), (), s32[]{:S(2)}) async-start(), calls=%async_computation.12 | async-start | bytes 2985984 | tf_op jit(solution)/shard_map/all_gather | solution.py:121
  106.1 80.2 %all-gather.9.cloned.1.call-start = ((), (), s32[]{:S(2)}) async-start(), calls=%async_computation.11 | async-start | bytes 2119680 | tf_op jit(solution)/shard_map/all_gather | solution.py:44
  147.8 77.8 %all-gather.15.cloned.1.call-start = ((), (), s32[]{:S(2)}) async-start(), calls=%async_computation.14 | async-start | bytes 2119680 | tf_op jit(solution)/shard_map/all_gather | solution.py:44
  148.4 108.1 %all-gather.13.cloned.1.call-start = ((), (), s32[]{:S(2)}) async-start(), calls=%async_computation.13 | async-start | bytes 2985984 | tf_op jit(solution)/shard_map/all_gather | solution.py:122
  149.1 158.2 %reduce-scatter.39.cloned.1.call-start = ((), (), s32[]{:S(2)}) async-start(), calls=%async_computation.24 | async-start | bytes 2119680
  256.5 9.4 %copy-start.24 = (bf16[1152,1076]{1,0:T(8,128)(2,1)S(1)}, bf16[1152,1076]{1,0:T(8,128)(2,1)}, u32[]{:S(2)}) copy-start(bf16[1152,1076]{1,0:T(8,128)(2,1)} %all-gather.11.cloned.1.call-done) | copy-start | bytes 7437316
  269.9 37.4 %copy-start.2 = (bf16[1,184,1152]{2,1,0:T(8,128)(2,1)S(1)}, bf16[1,184,1152]{2,1,0:T(8,128)(2,1)}, u32[]{:S(2)}) copy-start(bf16[1,184,1152]{2,1,0:T(8,128)(2,1)} %reduce-scatter.35.cloned.1.call-done) | copy-start | bytes 1271812
  269.9 76.4 %reduce-scatter.37.cloned.1.call-start = ((), (), s32[]{:S(2)}) async-start(), calls=%async_computation.23 | async-start | bytes 2119680
  277.2 111.3 %all-gather.17.cloned.1.call-start = ((), (), s32[]{:S(2)}) async-start(), calls=%async_computation.15 | async-start | bytes 2119680 | tf_op jit(solution)/shard_map/all_gather | solution.py:44
  348.9 43.2 %copy-start.22 = (f32[4,736]{1,0:T(4,128)S(1)}, f32[4,736]{1,0:T(4,128)}, u32[]{:S(2)}) copy-start(f32[4,736]{1,0:T(4,128)} %copy-done.21) | copy-start | bytes 35332
  349.8 96.9 %reduce-scatter.41.cloned.1.call-start = ((), (), s32[]{:S(2)}) async-start(), calls=%async_computation.25 | async-start | bytes 2119680
  392.1 5.7 copy-start.28
  397.8 10.6 %copy-start.14 = (bf16[736,4,72]{0,2,1:T(8,128)(2,1)}, bf16[736,4,72]{0,2,1:T(8,128)(2,1)S(1)}, u32[]{:S(2)}) copy-start(bf16[736,4,72]{0,2,1:T(8,128)(2,1)S(1)} %get-tuple-element.109) | copy-start | bytes 1271812
  397.8 5.6 copy-start.10
  410.8 97.0 %reduce-scatter.33.cloned.1.call-start = ((), (), s32[]{:S(2)}) async-start(), calls=%async_computation.21 | async-start | bytes 5971968 | tf_op jit(solution)/shard_map/reduce_scatter | solution.py:235
  418.2 150.6 %reduce-scatter.31.cloned.1.call-start = ((), (), s32[]{:S(2)}) async-start(), calls=%async_computation.20 | async-start | bytes 5971968 | tf_op jit(solution)/shard_map/reduce_scatter | solution.py:234
  426.2 5.0 copy-start.15
  426.2 185.7 %reduce-scatter.29.cloned.1.call-start = ((), (), s32[]{:S(2)}) async-start(), calls=%async_computation.19 | async-start | bytes 1990656 | tf_op jit(solution)/shard_map/reduce_scatter | solution.py:233
  431.1 4.1 copy-start.6
  431.1 223.9 %reduce-scatter.27.cloned.1.call-start = ((), (), s32[]{:S(2)}) async-start(), calls=%async_computation.18 | async-start | bytes 1990656 | tf_op jit(solution)/shard_map/reduce_scatter | solution.py:232
  435.1 4.1 copy-start.12
  435.1 263.1 %reduce-scatter.23.cloned.1.call-start = ((), (), s32[]{:S(2)}) async-start(), calls=%async_computation.16 | async-start | bytes 1990656 | tf_op jit(solution)/shard_map/reduce_scatter | solution.py:230
  439.1 3.9 copy-start.23
  439.1 302.3 %reduce-scatter.25.cloned.1.call-start = ((), (), s32[]{:S(2)}) async-start(), calls=%async_computation.17 | async-start | bytes 1990656 | tf_op jit(solution)/shard_map/reduce_scatter | solution.py:231
  (14 other events, 26.0 us)
Sparse Core Ops, SparseCore 0:
  49.1 38.4 all-gather.6
  105.7 37.5 reduce-scatter.34
  270.0 37.2 reduce-scatter.38
  309.5 36.7 reduce-scatter.36
  349.9 38.5 all-gather.16
Sparse Core Ops, SparseCore 1:
  107.9 30.3 all-gather.10
  147.9 38.4 all-gather.8
  187.8 37.8 all-gather.14
  227.5 28.9 all-gather.12
  410.9 35.8 reduce-scatter.40
  450.7 57.0 reduce-scatter.32
  512.0 56.7 reduce-scatter.30
  572.6 39.2 reduce-scatter.28
  615.7 39.2 reduce-scatter.26
  659.0 39.2 reduce-scatter.22
  702.1 39.2 reduce-scatter.24
